TPU v7x, 32 devices: a whole 2x2x4 slice. The times are simulated.
32 devices in a mesh: gx: 4 (over x, core), gy: 8 (over z, y).
Axes of the slice: x: 2, y: 2, z: 4, core: 2. Of those that a mesh axis runs over, the one named last changes fastest.
Arguments:
- blocks: float32 [8, 8, 9, 128, 128], P('gx', 'gy'), may hold values from -0.0625 to 0.0625
- pair_mask: int32 [8, 8, 9, 8, 8], P('gx', 'gy'), may hold values 0 or 1
- rhs_rows: float32 [8, 8, 9, 128, 128], P('gx', 'gy'), may hold values from -6 to 6
- counts: int32 [8, 8, 8], P('gx', 'gy'), may hold values from 1 to 3, as said below
Outputs:
- solution: float32 [8, 8, 9, 128, 128], P('gx', 'gy')
Inputs may be any that keep to these rules, and one draw needn't show every extreme that they name: `counts`: cut the first block index into runs of 2 blocks. Within each second index b, run a and run a + 2 together hold at most 2 blocks that have an atom with a count of 2 or more, and some run holds 2 such blocks; at least one atom takes 3 iterations and at least one takes 1.
All inputs are finite; a program needn't handle non-finite values. No bound on the sum of `pair_mask` on one device may be relied on, other than what follows from the above.
Results may differ from a plain program's by a relative error of at most 0.0003.
Values sent between devices are 32-bit elements; how exact they have to be, the bound alone decides.
A program may use at most 128 MiB of HBM per device.

v0:
```python
import jax
import jax.numpy as jnp
from jax import lax
from jax.sharding import PartitionSpec as P

ITERS = 3


def with_halo(block, sides, width):
    for axis, dim in sides:
        count = lax.axis_size(axis)
        forward = [(i, i + 1) for i in range(count - 1)]
        backward = [(target, source) for source, target in forward]
        low = lax.ppermute(
            lax.slice_in_dim(block, block.shape[dim] - width, None, axis=dim), axis, forward
        )
        high = lax.ppermute(lax.slice_in_dim(block, 0, width, axis=dim), axis, backward)
        block = jnp.concatenate([low, block, high], axis=dim)
    return block


def expand_mask(pair_mask, orbitals):
    shaped = pair_mask.astype(jnp.float32)[..., :, None, :, None]
    leading = pair_mask.shape[:-2]
    atom_count = pair_mask.shape[-1]
    expanded = jnp.broadcast_to(shaped, leading + (atom_count, orbitals, atom_count, orbitals))
    return expanded.reshape(leading + (atom_count * orbitals, atom_count * orbitals))


def cluster_apply(window, vectors):
    result = vectors
    for row_off in (-1, 0, 1):
        for col_off in (-1, 0, 1):
            offset = 3 * (row_off + 1) + (col_off + 1)
            row_low, row_high = (max(0, -row_off), min(3, 3 - row_off))
            col_low, col_high = (max(0, -col_off), min(3, 3 - col_off))
            coupled = window[..., row_low:row_high, col_low:col_high, offset, :, :]
            source = vectors[
                ...,
                row_low + row_off : row_high + row_off,
                col_low + col_off : col_high + col_off,
                :,
                :,
            ]
            product = jnp.einsum(
                "...xyij,...xyjc->...xyic", coupled, source, precision=lax.Precision.HIGHEST
            )
            result = result.at[..., row_low:row_high, col_low:col_high, :, :].add(-product)
    return result


def cluster_rhs(rhs_window):
    rows_list = []
    for row_pos in range(3):
        pieces = []
        for col_pos in range(3):
            pieces.append(rhs_window[..., row_pos, col_pos, 8 - 3 * row_pos - col_pos, :, :])
        rows_list.append(jnp.stack(pieces, axis=-3))
    return jnp.stack(rows_list, axis=-4)


def column_inner(left, other):
    return jnp.sum(left * other, axis=(-4, -3, -2))


def spread(scalar):
    return scalar[..., None, None, None, :]


def guarded(top, bottom, floor_val):
    return top * bottom / (bottom * bottom + floor_val * floor_val)


def start_state(window, right_side):
    image_first = cluster_apply(window, right_side)
    zero_field = jnp.zeros_like(right_side)
    norm_rhs = column_inner(right_side, right_side)
    zero_cols = jnp.zeros_like(norm_rhs)
    vectors = (right_side, right_side, right_side, image_first, image_first, zero_field, zero_field)
    scalars = (norm_rhs, 0.1 * norm_rhs, jnp.sqrt(norm_rhs), zero_cols, zero_cols, norm_rhs)
    return (vectors, scalars)


def iterate(window, vectors, scalars, iteration, limit_cols):
    shadow, residual, first_dir, image_first, vector, direction, solution = vectors
    rho_value, rho_floor, tau_value, theta_value, eta_value, norm_rhs = scalars
    alpha_floor = 0.1 * jnp.sqrt(norm_rhs * (column_inner(vector, vector) + 1e-06))
    alpha_value = guarded(rho_value, column_inner(shadow, vector), alpha_floor)
    step_ratio = guarded(1.0, alpha_value, 0.1)
    second = first_dir - spread(alpha_value) * vector
    image_second = cluster_apply(window, second)
    active = spread((limit_cols > iteration).astype(jnp.float32))
    for half_dir, half_image in ((first_dir, image_first), (second, image_second)):
        residual = residual - spread(alpha_value) * half_image
        direction = (
            half_dir + spread(theta_value * theta_value * eta_value * step_ratio) * direction
        )
        theta_value = jnp.sqrt(column_inner(residual, residual)) / tau_value
        cosine = 1.0 / jnp.sqrt(1.0 + theta_value * theta_value)
        tau_value = tau_value * theta_value * cosine
        eta_value = cosine * cosine * alpha_value
        solution = solution + active * spread(eta_value) * direction
    vectors = (shadow, residual, second, image_second, vector, direction, solution)
    scalars = (rho_value, rho_floor, tau_value, theta_value, eta_value, norm_rhs)
    return (vectors, scalars)


def advance(window, vectors, scalars):
    shadow, residual, second, image_second, vector, direction, solution = vectors
    rho_value, rho_floor, tau_value, theta_value, eta_value, norm_rhs = scalars
    rho_next = column_inner(shadow, residual)
    beta_value = guarded(rho_next, rho_value, rho_floor)
    next_floor = 0.1 * jnp.sqrt(norm_rhs * column_inner(residual, residual))
    first_dir = residual + spread(beta_value) * second
    image_first = cluster_apply(window, first_dir)
    vector = image_first + spread(beta_value) * (image_second + spread(beta_value) * vector)
    vectors = (shadow, residual, first_dir, image_first, vector, direction, solution)
    scalars = (rho_next, next_floor, tau_value, theta_value, eta_value, norm_rhs)
    return (vectors, scalars)


def first_section(window, right_side, limit_cols):
    vectors, scalars = start_state(window, right_side)
    return iterate(window, vectors, scalars, 0, limit_cols)


def later_section(window, vectors, scalars, limit_cols):
    for iteration in range(1, ITERS):
        vectors, scalars = advance(window, vectors, scalars)
        vectors, scalars = iterate(window, vectors, scalars, iteration, limit_cols)
    return vectors[6]


def shards(blocks, pair_mask, rhs_rows, counts):
    orbitals = blocks.shape[-1] // pair_mask.shape[-1]
    group_count = blocks.shape[0]
    rows_block = blocks.shape[-1]
    coupling = blocks * expand_mask(pair_mask, orbitals)
    padded_coupling, padded_rhs = (
        with_halo(coupling, (("gx", 0), ("gy", 1)), 1),
        with_halo(rhs_rows, (("gx", 0), ("gy", 1)), 1),
    )
    windows = jnp.stack(
        [padded_coupling[local_pos : local_pos + 3] for local_pos in range(group_count)]
    )
    rhs_windows = jnp.stack(
        [padded_rhs[local_pos : local_pos + 3] for local_pos in range(group_count)]
    )
    right_side = cluster_rhs(rhs_windows)
    limits = (
        jnp.repeat(counts, orbitals, axis=-1).reshape(group_count, rows_block).astype(jnp.float32)
    )
    vectors, scalars = first_section(windows, right_side, limits)
    solution = later_section(windows, vectors, scalars, limits)
    return solution.reshape(group_count, 1, 9, rows_block, solution.shape[-1])


def solution(mesh):
    return jax.shard_map(
        shards,
        mesh=mesh,
        in_specs=(
            P("gx", "gy", None, None, None),
            P("gx", "gy", None, None, None),
            P("gx", "gy", None, None, None),
            P("gx", "gy", None),
        ),
        out_specs=P("gx", "gy", None, None, None),
        check_vma=False,
    )
```

profile of v0, /device:TPU:25, one launch (start us, length us, event | category | flops | bytes accessed | tf_op | source)
XLA Modules:
  0.0 310.1 jit_solution(17595724895426408822)
XLA Ops:
  1.0 4.3 %broadcast_in_dim.14 = f32[2,9,8,16,8,16]{5,4,3,2,0,1:T(8,128)} broadcast(f32[2,9,8,8]{3,2,0,1:T(8,128)S(1)} %copy.10), dimensions={0,1,2,4} | broadcast | bytes 1184256 | tf_op jit(solution)/shard_map/broadcast_in_dim | solution.py:26
  5.3 6.3 %broadcast_in_dim.15 = f32[2,1,9,128,128]{4,3,1,0,2:T(8,128)S(1)} reshape(f32[2,9,8,16,8,16]{5,4,3,2,0,1:T(8,128)} %broadcast_in_dim.14) | data formatting | bytes 2359296 | tf_op jit(solution)/shard_map/broadcast_in_dim | solution.py:26
  11.9 3.7 %collective-permute-start.4 = (f32[1,1,9,128,128]{4,3,1,0,2:T(8,128)S(1)}, f32[1,1,9,128,128]{4,3,1,0,2:T(8,128)S(1)}, u32[]{:S(2)}, u32[]{:S(2)}) collective-permute-start(f32[1,1,9,128,128]{4,3,1,0,2:T(8,128)S(1)} %get-tuple-element.765), channel_id=1, source_target_pairs={{0,8},{8,16},{16,24},{1,9},{9,17},{17,25},{2,10},{10,18},{18,26},{... | collective-permute-start | bytes 1769480 | tf_op jit(solution)/shard_map/ppermute | solution.py:14
  15.6 2.1 collective-permute-start.5
  17.7 4.7 %collective-permute-done.4 = f32[1,1,9,128,128]{4,3,1,0,2:T(8,128)S(1)} collective-permute-done((f32[1,1,9,128,128]{4,3,1,0,2:T(8,128)S(1)}, f32[1,1,9,128,128]{4,3,1,0,2:T(8,128)S(1)}, u32[]{:S(2)}, u32[]{:S(2)}) %collective-permute-start.4) | collective-permute-done | bytes 589856 | tf_op jit(solution)/shard_map/ppermute | solution.py:14
  22.4 4.5 %collective-permute-done.5 = f32[1,1,9,128,128]{4,3,1,0,2:T(8,128)S(1)} collective-permute-done((f32[1,1,9,128,128]{4,3,1,0,2:T(8,128)S(1)}, f32[1,1,9,128,128]{4,3,1,0,2:T(8,128)S(1)}, u32[]{:S(2)}, u32[]{:S(2)}) %collective-permute-start.5) | collective-permute-done | bytes 589856 | tf_op jit(solution)/shard_map/ppermute | solution.py:17
  27.0 1.7 pad_maximum_fusion.2
  28.6 3.5 %collective-permute-start.6 = (f32[4,1,9,128,128]{4,3,1,0,2:T(8,128)}, f32[4,1,9,128,128]{4,3,1,0,2:T(8,128)}, u32[]{:S(2)}, u32[]{:S(2)}) collective-permute-start(f32[4,1,9,128,128]{4,3,1,0,2:T(8,128)} %pad_maximum_fusion.2), channel_id=1, source_target_pairs={{0,1},{1,2},{2,3},{3,4},{4,5},{5,6},{6,7},{8,9},{9,10},{10,11},{11... | collective-permute-start | bytes 7077896 | tf_op jit(solution)/shard_map/ppermute | solution.py:14
  32.2 2.6 collective-permute-start.7
  34.9 2.3 collective-permute-start
  37.2 2.1 collective-permute-start.1
  39.3 4.7 %collective-permute-done = f32[1,1,9,128,128]{4,3,2,1,0:T(8,128)S(1)} collective-permute-done((f32[1,1,9,128,128]{4,3,2,1,0:T(8,128)S(1)}, f32[1,1,9,128,128]{4,3,2,1,0:T(8,128)S(1)}, u32[]{:S(2)}, u32[]{:S(2)}) %collective-permute-start) | collective-permute-done | bytes 589856 | tf_op jit(solution)/shard_map/ppermute | solution.py:14
  46.1 2.8 collective-permute-done.1
  49.7 3.8 %collective-permute-start.2 = (f32[4,1,9,128,128]{4,3,2,1,0:T(8,128)}, f32[4,1,9,128,128]{4,3,2,1,0:T(8,128)}, u32[]{:S(2)}, u32[]{:S(2)}) collective-permute-start(f32[4,1,9,128,128]{4,3,2,1,0:T(8,128)} %constant_dynamic-update-slice_fusion.12), channel_id=1, source_target_pairs={{0,1},{1,2},{2,3},{3,4},{4,5},{5,6},{6,7},{8,9},{9,10},{10,11},{11... | collective-permute-start | bytes 7077896 | tf_op jit(solution)/shard_map/ppermute | solution.py:14
  53.5 2.4 collective-permute-start.3
  57.0 28.0 %collective-permute-done.6 = f32[4,1,9,128,128]{4,3,1,0,2:T(8,128)} collective-permute-done((f32[4,1,9,128,128]{4,3,1,0,2:T(8,128)}, f32[4,1,9,128,128]{4,3,1,0,2:T(8,128)}, u32[]{:S(2)}, u32[]{:S(2)}) %collective-permute-start.6) | collective-permute-done | bytes 2359328 | tf_op jit(solution)/shard_map/ppermute | solution.py:14
  85.0 94.4 %collective-permute-done.7 = f32[4,1,9,128,128]{4,3,1,0,2:T(8,128)} collective-permute-done((f32[4,1,9,128,128]{4,3,1,0,2:T(8,128)}, f32[4,1,9,128,128]{4,3,1,0,2:T(8,128)}, u32[]{:S(2)}, u32[]{:S(2)}) %collective-permute-start.7) | collective-permute-done | bytes 2359328 | tf_op jit(solution)/shard_map/ppermute | solution.py:17
  179.4 5.2 %pad_maximum_fusion.1 = f32[4,3,9,128,128]{4,3,1,0,2:T(8,128)} fusion(f32[4,1,9,128,128]{4,3,1,0,2:T(8,128)} %collective-permute-done.7, f32[1,1,9,128,128]{4,3,1,0,2:T(8,128)S(1)} %collective-permute-done.5, f32[2,1,9,128,128]{4,3,1,0,2:T(8,128)S(1)} %copy_multiply_fusion, f32[1,1,9,128,128]{4,3,1,0,2:T(8,128)S(1)} %collective-permute-done.4, ...), kind=kLoop, calls=%fused_computation.1 | loop fusion | flops 7077888 | bytes 14155776 | tf_op jit(solution)/shard_map/concatenate | solution.py:18
  184.6 5.0 %slice_bitcast_fusion.1 = (f32[1,3,3,9,128,128]{5,4,2,1,0,3:T(8,128)S(1)}, f32[1,3,3,9,128,128]{5,4,2,1,0,3:T(8,128)S(1)}) fusion(f32[4,3,9,128,128]{4,3,1,0,2:T(8,128)} %pad_maximum_fusion.1), kind=kLoop, calls=%fused_computation.3 | loop fusion | bytes 21233664 | tf_op jit(solution)/shard_map/stack | solution.py:143
  190.6 1.4 maximum_bitcast_fusion.2
  193.4 36.3 %collective-permute-done.3 = f32[4,1,9,128,128]{4,3,2,1,0:T(8,128)} collective-permute-done((f32[4,1,9,128,128]{4,3,2,1,0:T(8,128)}, f32[4,1,9,128,128]{4,3,2,1,0:T(8,128)}, u32[]{:S(2)}, u32[]{:S(2)}) %collective-permute-start.3) | collective-permute-done | bytes 2359328 | tf_op jit(solution)/shard_map/ppermute | solution.py:17
  229.7 3.6 %pad_maximum_fusion = f32[4,3,9,128,128]{4,3,2,1,0:T(8,128)S(1)} fusion(f32[4,1,9,128,128]{4,3,2,1,0:T(8,128)} %collective-permute-done.3, f32[4,1,9,128,128]{4,3,2,1,0:T(8,128)} %constant_dynamic-update-slice_fusion.12, f32[4,1,9,128,128]{4,3,2,1,0:T(8,128)} %collective-permute-done.2), kind=kLoop, calls=%fused_computation | loop fusion | flops 3538944 | bytes 14155776 | tf_op jit(solution)/shard_map/concatenate | solution.py:18
  233.3 5.3 %slice_bitcast_fusion.3 = (f32[1,3,3,9,128,128]{5,4,0,3,2,1:T(8,128)}, f32[1,3,3,9,128,128]{5,4,0,3,2,1:T(8,128)}) fusion(f32[4,3,9,128,128]{4,3,2,1,0:T(8,128)S(1)} %pad_maximum_fusion), kind=kLoop, calls=%fused_computation.5 | loop fusion | bytes 21233664 | tf_op jit(solution)/shard_map/stack | solution.py:146
  238.7 1.4 maximum_bitcast_fusion.16
  249.4 1.8 fusion.85
  261.2 1.9 fusion.77
  271.8 1.8 fusion.69
  279.7 1.6 fusion.2
  282.5 1.8 fusion.61
  293.1 1.8 fusion.53
  304.0 1.8 fusion.45
  308.1 1.9 multiply_add_fusion
  (142 shorter events, 61.8 us)
Async XLA Ops:
  5.3 6.3 %copy-start.10 = (f32[2,1,9,128,128]{4,3,2,1,0:T(8,128)S(1)}, f32[2,1,9,128,128]{4,3,2,1,0:T(8,128)}, u32[]{:S(2)}) copy-start(f32[2,1,9,128,128]{4,3,2,1,0:T(8,128)} %param.124) | copy-start | bytes 3538948
  11.9 10.5 %collective-permute-start.4 = (f32[1,1,9,128,128]{4,3,1,0,2:T(8,128)S(1)}, f32[1,1,9,128,128]{4,3,1,0,2:T(8,128)S(1)}, u32[]{:S(2)}, u32[]{:S(2)}) collective-permute-start(f32[1,1,9,128,128]{4,3,1,0,2:T(8,128)S(1)} %get-tuple-element.765), channel_id=1, source_target_pairs={{0,8},{8,16},{16,24},{1,9},{9,17},{17,25},{2,10},{10,18},{18,26},{... | collective-permute-start | bytes 1769480 | tf_op jit(solution)/shard_map/ppermute | solution.py:14
  15.6 19.2 %copy-start.9 = (f32[2,1,9,128,128]{4,3,2,1,0:T(8,128)S(1)}, f32[2,1,9,128,128]{4,3,2,1,0:T(8,128)}, u32[]{:S(2)}) copy-start(f32[2,1,9,128,128]{4,3,2,1,0:T(8,128)} %param.126) | copy-start | bytes 3538948
  15.6 11.3 %collective-permute-start.5 = (f32[1,1,9,128,128]{4,3,1,0,2:T(8,128)S(1)}, f32[1,1,9,128,128]{4,3,1,0,2:T(8,128)S(1)}, u32[]{:S(2)}, u32[]{:S(2)}) collective-permute-start(f32[1,1,9,128,128]{4,3,1,0,2:T(8,128)S(1)} %get-tuple-element.766), channel_id=1, source_target_pairs={{8,0},{16,8},{24,16},{9,1},{17,9},{25,17},{10,2},{18,10},{26,18},{... | collective-permute-start | bytes 1769480 | tf_op jit(solution)/shard_map/ppermute | solution.py:17
  28.6 56.4 %collective-permute-start.6 = (f32[4,1,9,128,128]{4,3,1,0,2:T(8,128)}, f32[4,1,9,128,128]{4,3,1,0,2:T(8,128)}, u32[]{:S(2)}, u32[]{:S(2)}) collective-permute-start(f32[4,1,9,128,128]{4,3,1,0,2:T(8,128)} %pad_maximum_fusion.2), channel_id=1, source_target_pairs={{0,1},{1,2},{2,3},{3,4},{4,5},{5,6},{6,7},{8,9},{9,10},{10,11},{11... | collective-permute-start | bytes 7077896 | tf_op jit(solution)/shard_map/ppermute | solution.py:14
  32.2 147.2 %collective-permute-start.7 = (f32[4,1,9,128,128]{4,3,1,0,2:T(8,128)}, f32[4,1,9,128,128]{4,3,1,0,2:T(8,128)}, u32[]{:S(2)}, u32[]{:S(2)}) collective-permute-start(f32[4,1,9,128,128]{4,3,1,0,2:T(8,128)} %pad_maximum_fusion.2), channel_id=1, source_target_pairs={{1,0},{2,1},{3,2},{4,3},{5,4},{6,5},{7,6},{9,8},{10,9},{11,10},{12... | collective-permute-start | bytes 7077896 | tf_op jit(solution)/shard_map/ppermute | solution.py:17
  34.9 9.1 %collective-permute-start = (f32[1,1,9,128,128]{4,3,2,1,0:T(8,128)S(1)}, f32[1,1,9,128,128]{4,3,2,1,0:T(8,128)S(1)}, u32[]{:S(2)}, u32[]{:S(2)}) collective-permute-start(f32[1,1,9,128,128]{4,3,2,1,0:T(8,128)S(1)} %get-tuple-element.768), channel_id=1, source_target_pairs={{0,8},{8,16},{16,24},{1,9},{9,17},{17,25},{2,10},{10,18},{18,26},{... | collective-permute-start | bytes 1769480 | tf_op jit(solution)/shard_map/ppermute | solution.py:14
  37.2 11.6 %collective-permute-start.1 = (f32[1,1,9,128,128]{4,3,2,1,0:T(8,128)S(1)}, f32[1,1,9,128,128]{4,3,2,1,0:T(8,128)S(1)}, u32[]{:S(2)}, u32[]{:S(2)}) collective-permute-start(f32[1,1,9,128,128]{4,3,2,1,0:T(8,128)S(1)} %get-tuple-element.767), channel_id=1, source_target_pairs={{8,0},{16,8},{24,16},{9,1},{17,9},{25,17},{10,2},{18,10},{26,18},{... | collective-permute-start | bytes 1769480 | tf_op jit(solution)/shard_map/ppermute | solution.py:17
  46.1 9.8 %copy-start.11 = (s32[2,1,8]{2,1,0:T(1,128)S(1)}, s32[2,1,8]{2,1,0:T(1,128)}, u32[]{:S(2)}) copy-start(s32[2,1,8]{2,1,0:T(1,128)} %param.127) | copy-start | bytes 196
  49.7 143.7 %collective-permute-start.2 = (f32[4,1,9,128,128]{4,3,2,1,0:T(8,128)}, f32[4,1,9,128,128]{4,3,2,1,0:T(8,128)}, u32[]{:S(2)}, u32[]{:S(2)}) collective-permute-start(f32[4,1,9,128,128]{4,3,2,1,0:T(8,128)} %constant_dynamic-update-slice_fusion.12), channel_id=1, source_target_pairs={{0,1},{1,2},{2,3},{3,4},{4,5},{5,6},{6,7},{8,9},{9,10},{10,11},{11... | collective-permute-start | bytes 7077896 | tf_op jit(solution)/shard_map/ppermute | solution.py:14
  53.5 176.3 %collective-permute-start.3 = (f32[4,1,9,128,128]{4,3,2,1,0:T(8,128)}, f32[4,1,9,128,128]{4,3,2,1,0:T(8,128)}, u32[]{:S(2)}, u32[]{:S(2)}) collective-permute-start(f32[4,1,9,128,128]{4,3,2,1,0:T(8,128)} %constant_dynamic-update-slice_fusion.12), channel_id=1, source_target_pairs={{1,0},{2,1},{3,2},{4,3},{5,4},{6,5},{7,6},{9,8},{10,9},{11,10},{12... | collective-permute-start | bytes 7077896 | tf_op jit(solution)/shard_map/ppermute | solution.py:17
  190.6 60.6 %copy-start = (f32[2,2,3,128,128]{4,3,2,1,0:T(8,128)}, f32[2,2,3,128,128]{4,3,2,1,0:T(8,128)S(1)}, u32[]{:S(2)}) copy-start(f32[2,2,3,128,128]{4,3,2,1,0:T(8,128)S(1)} %get-tuple-element.746) | copy-start | bytes 2359300
  240.3 1.0 copy-start.8
  241.3 1.1 copy-start.4
  243.4 1.0 copy-start.7
  244.5 1.1 copy-start.3
  246.8 1.4 copy-start.2
  248.2 1.2 copy-start.6
  252.2 1.0 copy-start.5
  261.2 1.9 copy-start.1
where the time goes:
time: 314 us; the launch traced here: 310 us
  waiting for transfers between devices  175 us (56%)
  matrix products  57.9 us (18%)
  local copies, waits for them, and re-layouts  30.6 us (10%)
  starting transfers between devices  22.4 us (7%)
  other arithmetic  22.1 us (7%)
    ppermute x4, waiting for transfers between devices, with_halo(): lax.ppermute(lax.slice_in_dim(block, 0, width, axis=dim), axis, backward)  138 us
    dot_general x54, matrix products, cluster_apply(): jnp.einsum('...xyij,...xyjc->...xyic', coupled, source, precision=lax.Pre...  57.9 us
    ppermute x4, waiting for transfers between devices, with_halo(): lax.ppermute(lax.slice_in_dim(block, block.shape[dim] - width, None, axis...  37.4 us
    ppermute x4, starting transfers between devices, with_halo(): lax.ppermute(lax.slice_in_dim(block, block.shape[dim] - width, None, axis...  13.3 us
    broadcast_in_dim x3, local copies, waits for them, and re-layouts, expand_mask(): jnp.broadcast_to(shaped, leading + (atom_count, orbitals, atom_count, orb...  10.8 us
    concatenate x3, other arithmetic, with_halo(): block = jnp.concatenate([low, block, high], axis=dim)  10.4 us
    ppermute x4, starting transfers between devices, with_halo(): lax.ppermute(lax.slice_in_dim(block, 0, width, axis=dim), axis, backward)  9.16 us
    unnamed x34, local copies, waits for them, and re-layouts  6.41 us
  transfers between devices with their start and end apart: 8, of which 7 were waited for; matrix products, arithmetic and copies ran while one was open for 6% of the time, Pallas kernels for 0%

commit v1 on v0

v1 whole, which is shorter than its diff:
```python
import functools

import jax
import jax.numpy as jnp
from jax import lax
from jax.experimental import pallas as pl
from jax.experimental.pallas import tpu as pltpu
from jax.sharding import PartitionSpec as P

ITERS = 3
MESH = pl.DeviceIdType.MESH
F32 = jnp.float32
BF16 = jnp.bfloat16
CHUNK = 64


def guarded(top, bottom, floor_val):
    return top * bottom / (bottom * bottom + floor_val * floor_val)


def split(value):
    high = value.astype(BF16)
    return high, (value - high.astype(F32)).astype(BF16)


def kernel(
    blocks, masks, rhs, limits, out,
    own_c, gy_c, gx_c, dg_c, gy_m, gx_m, dg_m, gy_r,
    mid, edge, v_hi, v_lo, res,
    shadow, w_vec, y_first, y_second, u_first, u_second, vec, direc, sol,
    send_sem, recv_sem, local_sem,
):
    b = blocks.shape[-1]
    orb = b // masks.shape[-2]
    strip = 3 * b
    rows = 9 * b
    gx, gy = lax.axis_index("gx"), lax.axis_index("gy")
    ngx, ngy = lax.axis_size("gx"), lax.axis_size("gy")
    gx_to = (gx < ngx - 1, gx > 0)
    gx_from = (gx > 0, gx < ngx - 1)
    gy_to = (gy < ngy - 1, gy > 0)
    gy_from = (gy > 0, gy < ngy - 1)
    gx_dev = ((gx + 1, gy), (gx - 1, gy))
    gy_dev = ((gx, gy + 1), (gx, gy - 1))

    def place(ref, group, row_off, col_off):
        return ref.at[
            pl.ds(strip * (row_off + 1) + b * (col_off + 1), b), pl.ds(b * group, b)
        ]

    count = [0]

    def remote(src, dst, device):
        number = count[0]
        count[0] += 1
        return pltpu.make_async_remote_copy(
            src_ref=src, dst_ref=dst, send_sem=send_sem.at[number],
            recv_sem=recv_sem.at[number], device_id=device, device_id_type=MESH,
        )

    row_of = (1, 0)
    ou_of = (1, 0)
    ov_of = (1, 0)
    far = (2, 0)
    pairs = ((0, 0, 1, 0), (0, 1, 2, -1), (1, 0, 0, 1), (1, 1, 1, 0))

    gy_early, gy_late, gx_direct, diag = {}, {}, {}, {}
    for t in (0, 1):
        early, late = [], []
        ov = far[t]
        early.append(remote(
            masks.at[:, :, pl.ds(ov_of[t], 2)], gy_m.at[t], gy_dev[t]))
        for s in (0, 1):
            early.append(remote(
                rhs.at[row_of[s], far[s], ov], gy_r.at[t, s], gy_dev[t]))
        for s in (0, 1):
            early.append(remote(
                blocks.at[row_of[s], pl.ds(ou_of[s], 2), pl.ds(ov_of[t], 2)],
                gy_c.at[t, row_of[s], pl.ds(ou_of[s], 2)], gy_dev[t]))
        for row, group, ou, row_off in pairs:
            late.append(remote(
                rhs.at[row, ou, ov], place(shadow, group, row_off, 2 * t - 1), gy_dev[t]))
        for s in (0, 1):
            ou = 2 - far[s]
            late.append(remote(
                blocks.at[row_of[s], ou, pl.ds(ov_of[t], 2)],
                gy_c.at[t, row_of[s], ou], gy_dev[t]))
        gy_early[t], gy_late[t] = early, late
    for s in (0, 1):
        row_off = 2 * s - 1
        gx_direct[s] = [
            remote(rhs.at[row_of[s], far[s], 1], place(shadow, s, row_off, 0), gx_dev[s]),
            remote(masks.at[row_of[s], pl.ds(ou_of[s], 2)], gx_m.at[s], gx_dev[s]),
            remote(blocks.at[row_of[s], pl.ds(ou_of[s], 2)], gx_c.at[s], gx_dev[s]),
        ]
        for t in (0, 1):
            diag[s, t] = [
                remote(gy_r.at[t, s], place(shadow, s, row_off, 2 * t - 1), gx_dev[s]),
                remote(gy_m.at[t, row_of[s], pl.ds(ou_of[s], 2)], dg_m.at[s, t], gx_dev[s]),
                remote(gy_c.at[t, row_of[s], pl.ds(ou_of[s], 2)], dg_c.at[s, t], gx_dev[s]),
            ]

    barrier = pltpu.get_barrier_semaphore()
    total = jnp.int32(0)
    for exists, device in zip(gx_to + gy_to, gx_dev + gy_dev):
        total = total + exists.astype(jnp.int32)

        @pl.when(exists)
        def _(device=device):
            pl.semaphore_signal(barrier, inc=1, device_id=device, device_id_type=MESH)
    pl.semaphore_wait(barrier, total)

    def start(condition, copies):
        @pl.when(condition)
        def _():
            for copy in copies:
                copy.start()

    for t in (0, 1):
        start(gy_to[t], gy_early[t])
    for s in (0, 1):
        start(gx_to[s], gx_direct[s])
    for t in (0, 1):
        start(gy_to[t], gy_late[t])

    locals_ = [pltpu.make_async_copy(blocks, own_c, local_sem.at[0])]
    for number, (row, group, ou, row_off) in enumerate(pairs):
        locals_.append(pltpu.make_async_copy(
            rhs.at[row, ou, 1], place(shadow, group, row_off, 0), local_sem.at[1 + number]))
    for copy in locals_:
        copy.start()

    def clear(ref):
        ref[...] = jnp.zeros(ref.shape, ref.dtype)

    def clear_rows(ref):
        def body(index, _):
            ref[pl.ds(index * b, b), :] = jnp.zeros((b, ref.shape[1]), ref.dtype)
            return 0
        lax.fori_loop(0, ref.shape[0] // b, body, 0)

    for ref in (u_second, vec, direc, sol):
        clear_rows(ref)
    clear_rows(v_hi)
    clear_rows(v_lo)
    zero = jnp.zeros((b, b), BF16)
    for ref in (mid, edge):
        for which in (0, 1):
            for part in (0, 1):
                for near in range(ref.shape[-1] // strip):
                    ref[which, part, 0:b, strip * near + 2 * b:strip * near + 3 * b] = zero
                    ref[which, part, 2 * b:3 * b, strip * near:strip * near + b] = zero

    def put(w, c, ou, ov, value, mask):
        masked = (value.reshape(b // orb, orb, b) * mask[:, None, :]).reshape(b, b)
        high, low = split(masked)
        base = (0, 0, 1, 2)[w]
        ref, which = ((edge, 0), (mid, 0), (mid, 1), (edge, 1))[w]
        col = strip * (w + ou - 1 - base) + b * (c + ov - 1)
        ref[which, 0, b * c:b * (c + 1), col:col + b] = high
        ref[which, 1, b * c:b * (c + 1), col:col + b] = low

    def finish(condition, copies, otherwise):
        @pl.when(condition)
        def _():
            for copy in copies:
                copy.wait_recv()

        @pl.when(jnp.logical_not(condition))
        def _():
            for ref in otherwise:
                clear(ref)

    locals_[0].wait()
    own_masks = limits[1]
    for row in (0, 1):
        for ou in range(3):
            for ov in range(3):
                put(row + 1, 1, ou, ov, own_c[row, ou, ov], own_masks[row, ou, ov])

    for t in (0, 1):
        @pl.when(gy_from[t])
        def _(t=t):
            for copy in gy_early[t]:
                copy.wait_recv()
        for s in (0, 1):
            start(jnp.logical_and(gy_from[t], gx_to[s]), diag[s, t])

    for s in (0, 1):
        finish(gx_from[s], gx_direct[s],
               [place(shadow, s, 2 * s - 1, 0), gx_m.at[s], gx_c.at[s]])
        for ou in range(2):
            for ov in range(3):
                put(3 * s, 1, ou + ou_of[s], ov, gx_c[s, ou, ov], gx_m[s, ou, ov])

    for t in (0, 1):
        @pl.when(jnp.logical_not(gy_from[t]))
        def _(t=t):
            clear(gy_m.at[t])
            for s in (0, 1):
                for ou in range(2):
                    for ov in range(2):
                        clear(gy_c.at[t, row_of[s], ou + ou_of[s], ov])
        for s in (0, 1):
            for ou in range(2):
                for ov in range(2):
                    at = (t, row_of[s], ou + ou_of[s], ov)
                    put(row_of[s] + 1, 2 * t, at[2], ov + ov_of[t], gy_c[at], gy_m[at])
    for t in (0, 1):
        for s in (0, 1):
            finish(jnp.logical_and(gx_from[s], gy_from[t]), diag[s, t],
                   [place(shadow, s, 2 * s - 1, 2 * t - 1), dg_m.at[s, t], dg_c.at[s, t]])
            for ou in range(2):
                for ov in range(2):
                    put(3 * s, 2 * t, ou + ou_of[s], ov + ov_of[t],
                        dg_c[s, t, ou, ov], dg_m[s, t, ou, ov])
    for copy in locals_[1:]:
        copy.wait()
    for t in (0, 1):
        finish(gy_from[t], gy_late[t],
               [place(shadow, group, row_off, 2 * t - 1) for _, group, _, row_off in pairs]
               + [gy_c.at[t, row_of[s], 2 - far[s]] for s in (0, 1)])
        for s in (0, 1):
            for ov in range(2):
                at = (t, row_of[s], 2 - far[s], ov)
                put(row_of[s] + 1, 2 * t, at[2], ov + ov_of[t], gy_c[at], gy_m[at])

    def over_chunks(body, sums):
        def step(index, carry):
            return body(pl.ds(pl.multiple_of(index * CHUNK, CHUNK), CHUNK), index * CHUNK, carry)
        return lax.fori_loop(
            0, rows // CHUNK, step, tuple(jnp.zeros((8, 2 * b), F32) for _ in range(sums)))

    def fold(value):
        return jnp.sum(value.reshape(CHUNK // 8, 8, 2 * b), axis=0)

    def column(value):
        return jnp.sum(value, axis=0, keepdims=True)

    def store_split(first, value):
        high, low = split(value)
        for ref, part in ((v_hi, high), (v_lo, low)):
            ref[pl.ds(pl.multiple_of(first, CHUNK), CHUNK), 0:b] = part[:, 0:b]
            ref[pl.ds(pl.multiple_of(first + strip, CHUNK), CHUNK), b:2 * b] = part[:, b:]

    def product(left, right):
        return jnp.dot(left, right, preferred_element_type=F32)

    def apply():
        for w in range(4):
            if w in (0, 3):
                which = w // 3
                near = pl.ds(2 * strip * which, 2 * strip)
                cols = slice(b * which, b * (which + 1))
                high, low = edge[which, 0], edge[which, 1]
            else:
                near = pl.ds(strip * (w - 1), 3 * strip)
                cols = slice(0, 2 * b)
                high, low = mid[w - 1, 0], mid[w - 1, 1]
            v_high, v_low = v_hi[near, cols], v_lo[near, cols]
            value = product(high, v_high) + product(low, v_high) + product(high, v_low)
            if w < 3:
                res[strip * w:strip * (w + 1), 0:b] = value[:, 0:b]
            if w > 0:
                res[strip * (w - 1):strip * w, b:2 * b] = value[:, -b:]

    def prepare(at, first, sums):
        value = shadow[at, :]
        w_vec[at, :] = value
        y_first[at, :] = value
        store_split(first, value)
        return (sums[0] + fold(value * value),)

    norm = column(over_chunks(prepare, 1)[0])
    limit = limits[0][...]

    def iteration(index, carry):
        rho, beta, tau, theta, eta, ratio = carry
        active = (limit > index.astype(F32)).astype(F32)
        apply()

        def after_first(at, first, sums):
            image = y_first[at, :] - res[at, :]
            u_first[at, :] = image
            value = image + beta * (u_second[at, :] + beta * vec[at, :])
            vec[at, :] = value
            return sums[0] + fold(value * value), sums[1] + fold(shadow[at, :] * value)

        square, along = (column(v) for v in over_chunks(after_first, 2))
        alpha = guarded(rho, along, 0.1 * jnp.sqrt(norm * (square + 1e-06)))
        ratio = guarded(1.0, alpha, 0.1)
        keep = theta * theta * eta * ratio

        def between(at, first, sums):
            y_one = y_first[at, :]
            residual = w_vec[at, :] - alpha * u_first[at, :]
            w_vec[at, :] = residual
            direc[at, :] = y_one + keep * direc[at, :]
            second = y_one - alpha * vec[at, :]
            y_second[at, :] = second
            store_split(first, second)
            return (sums[0] + fold(residual * residual),)

        size = column(over_chunks(between, 1)[0])

        def turn(size, tau):
            theta = jnp.sqrt(size) / tau
            cosine = 1.0 / jnp.sqrt(1.0 + theta * theta)
            return theta, tau * theta * cosine, cosine * cosine * alpha

        theta, tau, eta = turn(size, tau)
        eta_one = active * eta
        apply()

        def after_second(at, first, sums):
            image = y_second[at, :] - res[at, :]
            u_second[at, :] = image
            residual = w_vec[at, :] - alpha * image
            w_vec[at, :] = residual
            return sums[0] + fold(residual * residual), sums[1] + fold(shadow[at, :] * residual)

        size, rho_next = (column(v) for v in over_chunks(after_second, 2))
        keep = theta * theta * eta * ratio
        theta, tau, eta = turn(size, tau)
        eta_two = active * eta
        return keep, eta_one, eta_two, rho_next, size, tau, theta, eta, ratio

    def close(beta, keep, eta_one, eta_two):
        def body(at, first, sums):
            one, second = direc[at, :], y_second[at, :]
            two = second + keep * one
            direc[at, :] = two
            sol[at, :] = sol[at, :] + eta_one * one + eta_two * two
            value = w_vec[at, :] + beta * second
            y_first[at, :] = value
            store_split(first, value)
            return sums
        over_chunks(body, 0)

    zero_row = jnp.zeros_like(norm)

    def whole(index, carry):
        rho, floor, beta, tau, theta, eta, ratio = carry
        keep, eta_one, eta_two, rho_next, size, tau, theta, eta, ratio = iteration(
            index, (rho, beta, tau, theta, eta, ratio))
        beta = guarded(rho_next, rho, floor)
        floor = 0.1 * jnp.sqrt(norm * size)
        close(beta, keep, eta_one, eta_two)
        return rho_next, floor, beta, tau, theta, eta, ratio

    lax.fori_loop(0, ITERS, whole, (
        norm, 0.1 * norm, zero_row, jnp.sqrt(norm), zero_row, zero_row, zero_row))

    def write(index, _):
        at = pl.ds(pl.multiple_of(index * b, b), b)
        out[0, index] = sol[at, 0:b]
        out[1, index] = sol[at, b:2 * b]
        return 0

    lax.fori_loop(0, 9, write, 0)

    for t in (0, 1):
        for copies in (gy_early[t], gy_late[t]):
            @pl.when(gy_to[t])
            def _(copies=copies):
                for copy in copies:
                    copy.wait_send()
    for s in (0, 1):
        @pl.when(gx_to[s])
        def _(s=s):
            for copy in gx_direct[s]:
                copy.wait_send()
        for t in (0, 1):
            @pl.when(jnp.logical_and(gy_from[t], gx_to[s]))
            def _(s=s, t=t):
                for copy in diag[s, t]:
                    copy.wait_send()


def entry(*refs):
    blocks, masks, rhs, limits, own_masks, out, *scratch = refs
    kernel(blocks, masks, rhs, (limits, own_masks), out, *scratch)


def shards(blocks, pair_mask, rhs_rows, counts):
    groups = blocks.shape[0]
    b = blocks.shape[-1]
    atoms = pair_mask.shape[-1]
    orb = b // atoms
    blocks = blocks.reshape(groups, 3, 3, b, b)
    rhs = rhs_rows.reshape(groups, 3, 3, b, b)
    masks = jnp.repeat(pair_mask.astype(F32), orb, axis=-1).reshape(groups, 3, 3, atoms, b)
    limits = jnp.repeat(counts.astype(F32), orb, axis=-1).reshape(1, groups * b)
    field = pltpu.VMEM((9 * b, 2 * b), F32)
    any_spec = pl.BlockSpec(memory_space=pl.ANY)
    vmem_spec = pl.BlockSpec(memory_space=pltpu.VMEM)
    copies = 2 * 11 + 2 * 3 + 4 * 3
    solved = pl.pallas_call(
        entry,
        out_shape=jax.ShapeDtypeStruct((groups, 9, b, b), F32),
        in_specs=[any_spec, any_spec, any_spec, vmem_spec, vmem_spec],
        out_specs=vmem_spec,
        scratch_shapes=[
            pltpu.VMEM((groups, 3, 3, b, b), F32),
            pltpu.VMEM((2, groups, 3, 2, b, b), F32),
            pltpu.VMEM((2, 2, 3, b, b), F32),
            pltpu.VMEM((2, 2, 2, 2, b, b), F32),
            pltpu.VMEM((2, groups, 3, 2, atoms, b), F32),
            pltpu.VMEM((2, 2, 3, atoms, b), F32),
            pltpu.VMEM((2, 2, 2, 2, atoms, b), F32),
            pltpu.VMEM((2, 2, b, b), F32),
            pltpu.VMEM((2, 2, 3 * b, 9 * b), BF16),
            pltpu.VMEM((2, 2, 3 * b, 6 * b), BF16),
            pltpu.VMEM((12 * b, 2 * b), BF16),
            pltpu.VMEM((12 * b, 2 * b), BF16),
            field, field, field, field, field, field, field, field, field, field,
            pltpu.SemaphoreType.DMA((copies,)),
            pltpu.SemaphoreType.DMA((copies,)),
            pltpu.SemaphoreType.DMA((5,)),
        ],
        compiler_params=pltpu.CompilerParams(
            collective_id=0, has_side_effects=True, vmem_limit_bytes=60 * 1024 * 1024
        ),
    )(blocks, masks, rhs, limits, masks)
    return solved.reshape(groups, 1, 9, b, b)


def solution(mesh):
    spec = P("gx", "gy", None, None, None)
    return jax.shard_map(
        shards,
        mesh=mesh,
        in_specs=(spec, spec, spec, P("gx", "gy", None)),
        out_specs=spec,
        check_vma=False,
    )
```

time: 314 us -> 89.1 us (0.28)
  waiting for transfers between devices: 175 us -> 0 us
  Pallas kernels: 0 us -> 82.4 us
  matrix products: 57.9 us -> 0 us
  local copies, waits for them, and re-layouts: 30.6 us -> 4.34 us
  starting transfers between devices: 22.4 us -> 0 us
  other arithmetic: 22.1 us -> 1.53 us
    ppermute x8 -> x0, waiting for transfers between devices: 175 us -> none  [the longest x4 138 us: with_halo(): lax.ppermute(lax.slice_in_dim(block, 0, width, axis=dim), axis, backward)]
    pallas_call x0 -> x1, Pallas kernels: none -> 82.4 us  [shards(): pl.pallas_call(entry, out_shape=jax.ShapeDtypeStruct((groups, 9, b, b), F...]
    dot_general x54 -> x0, matrix products: 57.9 us -> none  [cluster_apply(): jnp.einsum('...xyij,...xyjc->...xyic', coupled, source, precision=lax.Pre...]
    ppermute x8 -> x0, starting transfers between devices: 22.4 us -> none  [the longest x4 13.3 us: with_halo(): lax.ppermute(lax.slice_in_dim(block, block.shape[dim] - width, None, axis...]
    concatenate x3 -> x0, other arithmetic: 10.4 us -> none  [with_halo(): block = jnp.concatenate([low, block, high], axis=dim)]
    another operation x6 -> x1, local copies, waits for them, and re-layouts: 10.9 us -> 0.66 us  [shards(): limits = jnp.repeat(counts.astype(F32), orb, axis=-1).reshape(1, groups * b)]
    broadcast_in_dim x6 -> x3, local copies, waits for them, and re-layouts: 11 us -> 1.14 us  [the longest x2 1.07 us: shards(): jnp.repeat(pair_mask.astype(F32), orb, axis=-1)]
    unnamed x34 -> x1, local copies, waits for them, and re-layouts: 6.41 us -> 2.39 us
  transfers between devices with their start and end apart: 8 -> 0, of which waited for: 7 -> 0; matrix products, arithmetic and copies ran while one was open for 6% -> 0% of each run, Pallas kernels for 0% -> 0%
where the time goes in v1:
time: 89.1 us; the launch traced here: 88.3 us
  Pallas kernels  82.4 us (92%)
  local copies, waits for them, and re-layouts  4.34 us (5%)
  other arithmetic  1.53 us (2%)
    pallas_call x1, Pallas kernels, shards(): pl.pallas_call(entry, out_shape=jax.ShapeDtypeStruct((groups, 9, b, b), F...  82.4 us
    unnamed x1, local copies, waits for them, and re-layouts  2.39 us

profile of v1, /device:TPU:25, one launch (start us, length us, event | category | flops | bytes accessed | tf_op | source)
XLA Modules:
  0.0 88.3 jit_solution(16092391712105393779)
XLA Ops:
  0.0 0.7 convert_element_type.12
  0.7 0.1 broadcast_in_dim.10
  0.8 0.7 reshape_reshape.4.refs_3_
  1.4 0.8 convert_bitcast_fusion
  2.3 0.2 copy.5
  2.4 0.2 broadcast_in_dim.8
  2.6 0.8 broadcast_in_dim.9.refs_1_.refs_4_
  3.5 82.4 %shard_map.46 = f32[2,9,128,128]{3,2,1,0:T(8,128)} custom-call(f32[2,3,3,128,128]{4,3,2,1,0:T(8,128)} %bitcast.15, f32[2,3,3,8,128]{4,3,2,1,0:T(8,128)} %broadcast_in_dim.9.refs_1_.refs_4_, f32[2,3,3,128,128]{4,3,2,1,0:T(8,128)} %bitcast.16, f32[1,256]{1,0:T(1,128)} %reshape_reshape.4.refs_3_, f32[2,3,3,8,128]{4,3,2,1,0:T(8,128)} %broadcast_in_dim.9.refs_1_.refs_4_), custom_call_target="tpu_custom_call" | custom-call | tf_op jit(solution)/shard_map/pallas_call | solution.py:398
  85.9 2.4 %copy.8 = f32[2,1,9,128,128]{4,3,2,1,0:T(8,128)} copy(f32[2,1,9,128,128]{4,3,2,1,0:T(8,128)} %bitcast.14) | data formatting | bytes 2359296

commit v2 on v1

--- a/solution.py
+++ b/solution.py
@@ -24,14 +24,15 @@
 
 
 def kernel(
-    blocks, masks, rhs, limits, out,
+    blocks, masks, rhs, limits, own_masks, out,
     own_c, gy_c, gx_c, dg_c, gy_m, gx_m, dg_m, gy_r,
     mid, edge, v_hi, v_lo, res,
     shadow, w_vec, y_first, y_second, u_first, u_second, vec, direc, sol,
     send_sem, recv_sem, local_sem,
 ):
     b = blocks.shape[-1]
-    orb = b // masks.shape[-2]
+    atoms = masks.shape[-1]
+    orb = b // atoms
     strip = 3 * b
     rows = 9 * b
     gx, gy = lax.axis_index("gx"), lax.axis_index("gy")
@@ -64,9 +65,9 @@
     far = (2, 0)
     pairs = ((0, 0, 1, 0), (0, 1, 2, -1), (1, 0, 0, 1), (1, 1, 1, 0))
 
-    gy_early, gy_late, gx_direct, diag = {}, {}, {}, {}
-    for t in (0, 1):
-        early, late = [], []
+    gy_early, gy_rhs, gy_late, gx_direct, diag = {}, {}, {}, {}, {}
+    for t in (0, 1):
+        early, right, late = [], [], []
         ov = far[t]
         early.append(remote(
             masks.at[:, :, pl.ds(ov_of[t], 2)], gy_m.at[t], gy_dev[t]))
@@ -78,14 +79,14 @@
                 blocks.at[row_of[s], pl.ds(ou_of[s], 2), pl.ds(ov_of[t], 2)],
                 gy_c.at[t, row_of[s], pl.ds(ou_of[s], 2)], gy_dev[t]))
         for row, group, ou, row_off in pairs:
-            late.append(remote(
+            right.append(remote(
                 rhs.at[row, ou, ov], place(shadow, group, row_off, 2 * t - 1), gy_dev[t]))
         for s in (0, 1):
             ou = 2 - far[s]
             late.append(remote(
                 blocks.at[row_of[s], ou, pl.ds(ov_of[t], 2)],
                 gy_c.at[t, row_of[s], ou], gy_dev[t]))
-        gy_early[t], gy_late[t] = early, late
+        gy_early[t], gy_rhs[t], gy_late[t] = early, right, late
     for s in (0, 1):
         row_off = 2 * s - 1
         gx_direct[s] = [
@@ -120,8 +121,12 @@
         start(gy_to[t], gy_early[t])
     for s in (0, 1):
         start(gx_to[s], gx_direct[s])
-    for t in (0, 1):
-        start(gy_to[t], gy_late[t])
+
+    def sent(condition, copies):
+        @pl.when(condition)
+        def _():
+            for copy in copies:
+                copy.wait_send()
 
     locals_ = [pltpu.make_async_copy(blocks, own_c, local_sem.at[0])]
     for number, (row, group, ou, row_off) in enumerate(pairs):
@@ -133,6 +138,14 @@
     def clear(ref):
         ref[...] = jnp.zeros(ref.shape, ref.dtype)
 
+    zero = jnp.zeros((b, b), BF16)
+    for group in (0, 1):
+        for part in (0, 1):
+            for t in (0, 1):
+                at = 2 * strip * (1 - group) + b * t
+                mid[group, part, 2 * b * t:2 * b * t + b, at:at + 2 * b] = jnp.zeros(
+                    (b, 2 * b), BF16)
+
     def clear_rows(ref):
         def body(index, _):
             ref[pl.ds(index * b, b), :] = jnp.zeros((b, ref.shape[1]), ref.dtype)
@@ -143,13 +156,22 @@
         clear_rows(ref)
     clear_rows(v_hi)
     clear_rows(v_lo)
-    zero = jnp.zeros((b, b), BF16)
     for ref in (mid, edge):
         for which in (0, 1):
             for part in (0, 1):
                 for near in range(ref.shape[-1] // strip):
                     ref[which, part, 0:b, strip * near + 2 * b:strip * near + 3 * b] = zero
                     ref[which, part, 2 * b:3 * b, strip * near:strip * near + b] = zero
+
+    spread = (
+        lax.broadcasted_iota(jnp.int32, (atoms, b), 1) // orb
+        == lax.broadcasted_iota(jnp.int32, (atoms, b), 0)
+    ).astype(F32)
+
+    def widen(value):
+        flat = value.astype(F32).reshape(-1, atoms)
+        wide = jnp.dot(flat, spread, preferred_element_type=F32)
+        return wide.reshape(value.shape[:-1] + (b,))
 
     def put(w, c, ou, ov, value, mask):
         masked = (value.reshape(b // orb, orb, b) * mask[:, None, :]).reshape(b, b)
@@ -172,26 +194,35 @@
                 clear(ref)
 
     locals_[0].wait()
-    own_masks = limits[1]
+    own_m = widen(own_masks[...])
     for row in (0, 1):
         for ou in range(3):
             for ov in range(3):
-                put(row + 1, 1, ou, ov, own_c[row, ou, ov], own_masks[row, ou, ov])
-
-    for t in (0, 1):
-        @pl.when(gy_from[t])
-        def _(t=t):
-            for copy in gy_early[t]:
-                copy.wait_recv()
-        for s in (0, 1):
+                put(row + 1, 1, ou, ov, own_c[row, ou, ov], own_m[row, ou, ov])
+
+    for t in (0, 1):
+        sent(gy_to[t], gy_early[t])
+        start(gy_to[t], gy_rhs[t])
+    for s in (0, 1):
+        for t in (0, 1):
+            @pl.when(gy_from[t])
+            def _(s=s, t=t):
+                if s == 0:
+                    gy_early[t][0].wait_recv()
+                gy_early[t][1 + s].wait_recv()
+                gy_early[t][3 + s].wait_recv()
             start(jnp.logical_and(gy_from[t], gx_to[s]), diag[s, t])
+    for t in (0, 1):
+        sent(gy_to[t], gy_rhs[t])
+        start(gy_to[t], gy_late[t])
 
     for s in (0, 1):
         finish(gx_from[s], gx_direct[s],
                [place(shadow, s, 2 * s - 1, 0), gx_m.at[s], gx_c.at[s]])
+        wide = widen(gx_m[s])
         for ou in range(2):
             for ov in range(3):
-                put(3 * s, 1, ou + ou_of[s], ov, gx_c[s, ou, ov], gx_m[s, ou, ov])
+                put(3 * s, 1, ou + ou_of[s], ov, gx_c[s, ou, ov], wide[ou, ov])
 
     for t in (0, 1):
         @pl.when(jnp.logical_not(gy_from[t]))
@@ -201,30 +232,26 @@
                 for ou in range(2):
                     for ov in range(2):
                         clear(gy_c.at[t, row_of[s], ou + ou_of[s], ov])
+        gy_wide = widen(gy_m[t])
         for s in (0, 1):
             for ou in range(2):
                 for ov in range(2):
                     at = (t, row_of[s], ou + ou_of[s], ov)
-                    put(row_of[s] + 1, 2 * t, at[2], ov + ov_of[t], gy_c[at], gy_m[at])
+                    put(row_of[s] + 1, 2 * t, at[2], ov + ov_of[t], gy_c[at], gy_wide[at[1:]])
     for t in (0, 1):
         for s in (0, 1):
             finish(jnp.logical_and(gx_from[s], gy_from[t]), diag[s, t],
                    [place(shadow, s, 2 * s - 1, 2 * t - 1), dg_m.at[s, t], dg_c.at[s, t]])
+            wide = widen(dg_m[s, t])
             for ou in range(2):
                 for ov in range(2):
                     put(3 * s, 2 * t, ou + ou_of[s], ov + ov_of[t],
-                        dg_c[s, t, ou, ov], dg_m[s, t, ou, ov])
+                        dg_c[s, t, ou, ov], wide[ou, ov])
     for copy in locals_[1:]:
         copy.wait()
     for t in (0, 1):
-        finish(gy_from[t], gy_late[t],
-               [place(shadow, group, row_off, 2 * t - 1) for _, group, _, row_off in pairs]
-               + [gy_c.at[t, row_of[s], 2 - far[s]] for s in (0, 1)])
-        for s in (0, 1):
-            for ov in range(2):
-                at = (t, row_of[s], 2 - far[s], ov)
-                put(row_of[s] + 1, 2 * t, at[2], ov + ov_of[t], gy_c[at], gy_m[at])
-
+        finish(gy_from[t], gy_rhs[t],
+               [place(shadow, group, row_off, 2 * t - 1) for _, group, _, row_off in pairs])
     def over_chunks(body, sums):
         def step(index, carry):
             return body(pl.ds(pl.multiple_of(index * CHUNK, CHUNK), CHUNK), index * CHUNK, carry)
@@ -272,12 +299,36 @@
         return (sums[0] + fold(value * value),)
 
     norm = column(over_chunks(prepare, 1)[0])
-    limit = limits[0][...]
+    limit = jnp.concatenate(
+        [widen(jnp.broadcast_to(limits[group], (atoms, atoms)))[0:1] for group in (0, 1)], axis=1)
+    apply()
+    for t in (0, 1):
+        finish(gy_from[t], gy_late[t],
+               [gy_c.at[t, row_of[s], 2 - far[s]] for s in (0, 1)])
+        gy_wide = widen(gy_m[t])
+        for s in (0, 1):
+            for ov in range(2):
+                at = (t, row_of[s], 2 - far[s], ov)
+                put(row_of[s] + 1, 2 * t, at[2], ov + ov_of[t], gy_c[at], gy_wide[at[1:]])
+    for group in (0, 1):
+        for t in (0, 1):
+            here = pl.ds(b * 2 * t, b)
+            cols = pl.ds(2 * strip * (1 - group) + b * t, 2 * b)
+            source = pl.ds(strip * (2 - group) + b * t, 2 * b)
+            v_high, v_low = v_hi[source, :], v_lo[source, :]
+            high, low = mid[group, 0, here, cols], mid[group, 1, here, cols]
+            value = product(high, v_high) + product(low, v_high) + product(high, v_low)
+            for k in (0, 1):
+                into, lanes = pl.ds(strip * (group + 1 - k) + b * 2 * t, b), pl.ds(b * k, b)
+                res[into, lanes] = res[into, lanes] + value[:, b * k:b * (k + 1)]
 
     def iteration(index, carry):
         rho, beta, tau, theta, eta, ratio = carry
         active = (limit > index.astype(F32)).astype(F32)
-        apply()
+
+        @pl.when(index > 0)
+        def _():
+            apply()
 
         def after_first(at, first, sums):
             image = y_first[at, :] - res[at, :]
@@ -360,44 +411,27 @@
     lax.fori_loop(0, 9, write, 0)
 
     for t in (0, 1):
-        for copies in (gy_early[t], gy_late[t]):
-            @pl.when(gy_to[t])
-            def _(copies=copies):
-                for copy in copies:
-                    copy.wait_send()
+        sent(gy_to[t], gy_late[t])
     for s in (0, 1):
-        @pl.when(gx_to[s])
-        def _(s=s):
-            for copy in gx_direct[s]:
-                copy.wait_send()
+        sent(gx_to[s], gx_direct[s])
         for t in (0, 1):
-            @pl.when(jnp.logical_and(gy_from[t], gx_to[s]))
-            def _(s=s, t=t):
-                for copy in diag[s, t]:
-                    copy.wait_send()
-
-
-def entry(*refs):
-    blocks, masks, rhs, limits, own_masks, out, *scratch = refs
-    kernel(blocks, masks, rhs, (limits, own_masks), out, *scratch)
+            sent(jnp.logical_and(gy_from[t], gx_to[s]), diag[s, t])
 
 
 def shards(blocks, pair_mask, rhs_rows, counts):
     groups = blocks.shape[0]
     b = blocks.shape[-1]
     atoms = pair_mask.shape[-1]
-    orb = b // atoms
     blocks = blocks.reshape(groups, 3, 3, b, b)
     rhs = rhs_rows.reshape(groups, 3, 3, b, b)
-    masks = jnp.repeat(pair_mask.astype(F32), orb, axis=-1).reshape(groups, 3, 3, atoms, b)
-    limits = jnp.repeat(counts.astype(F32), orb, axis=-1).reshape(1, groups * b)
+    masks = pair_mask.reshape(groups, 3, 3, atoms, atoms)
     field = pltpu.VMEM((9 * b, 2 * b), F32)
     any_spec = pl.BlockSpec(memory_space=pl.ANY)
     vmem_spec = pl.BlockSpec(memory_space=pltpu.VMEM)
     copies = 2 * 11 + 2 * 3 + 4 * 3
     solved = pl.pallas_call(
-        entry,
-        out_shape=jax.ShapeDtypeStruct((groups, 9, b, b), F32),
+        kernel,
+        out_shape=pltpu.VMEM((groups, 9, b, b), F32),
         in_specs=[any_spec, any_spec, any_spec, vmem_spec, vmem_spec],
         out_specs=vmem_spec,
         scratch_shapes=[
@@ -405,9 +439,9 @@
             pltpu.VMEM((2, groups, 3, 2, b, b), F32),
             pltpu.VMEM((2, 2, 3, b, b), F32),
             pltpu.VMEM((2, 2, 2, 2, b, b), F32),
-            pltpu.VMEM((2, groups, 3, 2, atoms, b), F32),
-            pltpu.VMEM((2, 2, 3, atoms, b), F32),
-            pltpu.VMEM((2, 2, 2, 2, atoms, b), F32),
+            pltpu.VMEM((2, groups, 3, 2, atoms, atoms), jnp.int32),
+            pltpu.VMEM((2, 2, 3, atoms, atoms), jnp.int32),
+            pltpu.VMEM((2, 2, 2, 2, atoms, atoms), jnp.int32),
             pltpu.VMEM((2, 2, b, b), F32),
             pltpu.VMEM((2, 2, 3 * b, 9 * b), BF16),
             pltpu.VMEM((2, 2, 3 * b, 6 * b), BF16),
@@ -421,7 +455,7 @@
         compiler_params=pltpu.CompilerParams(
             collective_id=0, has_side_effects=True, vmem_limit_bytes=60 * 1024 * 1024
         ),
-    )(blocks, masks, rhs, limits, masks)
+    )(blocks, masks, rhs, counts, masks)
     return solved.reshape(groups, 1, 9, b, b)
 
 

time: 89.1 us -> 83.7 us (0.939)
  Pallas kernels: 82.4 us -> 79.8 us
  local copies, waits for them, and re-layouts: 4.34 us -> 2.65 us
  other arithmetic: 1.53 us -> 0 us
    pallas_call x1, Pallas kernels: 82.4 us -> 79.8 us  [shards(): pl.pallas_call(kernel, out_shape=pltpu.VMEM((groups, 9, b, b), F32), in_s...]
    convert_element_type x2 -> x0, other arithmetic: 1.53 us -> none  [the longest x1 0.84 us: shards(): pair_mask.astype(F32)]
    broadcast_in_dim x3 -> x0, local copies, waits for them, and re-layouts: 1.14 us -> none  [the longest x2 1.07 us: shards(): jnp.repeat(pair_mask.astype(F32), orb, axis=-1)]
    unnamed x1 -> x2, local copies, waits for them, and re-layouts: 2.39 us -> 2.65 us
where the time goes in v2:
time: 83.7 us; the launch traced here: 82.4 us
  Pallas kernels  79.8 us (95%)
  local copies, waits for them, and re-layouts  2.65 us (3%)
    pallas_call x1, Pallas kernels, shards(): pl.pallas_call(kernel, out_shape=pltpu.VMEM((groups, 9, b, b), F32), in_s...  79.8 us
    unnamed x2, local copies, waits for them, and re-layouts  2.65 us

profile of v2, /device:TPU:25, one launch (start us, length us, event | category | flops | bytes accessed | tf_op | source)
XLA Modules:
  0.0 82.4 jit_solution(11194625700142952051)
XLA Ops:
  0.0 1.6 %copy.5 = s32[2,1,9,8,8]{4,3,2,0,1:T(8,128)} copy(s32[2,1,9,8,8]{2,4,3,1,0:T(8,128)} %param.5) | data formatting | bytes 9216 | tf_op args[1]
  1.6 79.8 %shard_map.46 = f32[2,9,128,128]{3,2,1,0:T(8,128)S(1)} custom-call(f32[2,3,3,128,128]{4,3,2,1,0:T(8,128)} %bitcast.7, s32[2,3,3,8,8]{4,3,2,1,0:T(8,128)} %bitcast.9, f32[2,3,3,128,128]{4,3,2,1,0:T(8,128)} %bitcast.8, s32[2,1,8]{2,1,0:T(1,128)} %limits.1, s32[2,3,3,8,8]{4,3,2,1,0:T(8,128)} %bitcast.10), custom_call_target="tpu_custom_call" | custom-call | tf_op jit(solution)/shard_map/pallas_call | solution.py:432
  81.4 1.0 %copy.8 = f32[2,1,9,128,128]{4,3,2,1,0:T(8,128)} copy(f32[2,1,9,128,128]{4,3,2,1,0:T(8,128)S(1)} %bitcast.6) | data formatting | bytes 2359296
